TPU v7x, 256 devices: a whole 4x4x8 slice. The times are simulated.
256 devices in a mesh: gx: 2 (over core), gy: 4 (over x), gz: 32 (over z, y).
Axes of the slice: x: 4, y: 4, z: 8, core: 2. Of those that a mesh axis runs over, the one named last changes fastest.
Arguments:
- resid_x: float32 [6, 8, 32, 120, 512], P('gx', 'gy', 'gz'), may hold values from -6 to 6
- resid_y: float32 [4, 12, 32, 120, 512], P('gx', 'gy', 'gz'), may hold values from -6 to 6
- face_weights: float32 [4, 8, 32, 4, 120], P('gx', 'gy', 'gz'), may hold values from 0.25 to 0.75
- face_counts: int32 [4, 8, 32, 4], P('gx', 'gy', 'gz'), may hold values from 1 to 4, as said below
- neumann: bfloat16 [4, 8, 32, 480, 480], P('gx', 'gy', 'gz'), may hold values from -0.25 to 0.25
- schur: bfloat16 [4, 8, 32, 480, 480], P('gx', 'gy', 'gz'), may hold values from -0.25 to 0.25
- basis: bfloat16 [4, 8, 32, 480, 64], P('gx', 'gy', 'gz'), may hold values from -0.25 to 0.25
- coarse_map: int32 [4, 8, 32, 64], P('gx', 'gy', 'gz'), may hold values from 0 to 511
- column_inverse: float32 [2, 4, 512, 512], P('gx', 'gy', 'gz'), may hold values from -0.25 to 0.25
- column_basis: float32 [2, 4, 512, 512], P('gx', 'gy', 'gz'), may hold values from -0.25 to 0.25
- top_inverse: float32 [512, 512], replicated, may hold values from -0.09375 to 0.09375
Outputs:
- z_x: float32 [6, 8, 32, 120, 512], P('gx', 'gy', 'gz')
- z_y: float32 [4, 12, 32, 120, 512], P('gx', 'gy', 'gz')
- schur_image: bfloat16 [4, 8, 32, 480, 512], P('gx', 'gy', 'gz')
Inputs may be any that keep to these rules, and one draw needn't show every extreme that they name: `face_counts`: only the first 30 * count of a face's 120 dofs are live; about one face in eight has 4 live mesh faces. `coarse_map`: several local coarse dofs may share a column coarse dof.
All inputs are finite; a program needn't handle non-finite values.
Results may differ from a plain program's by a relative error of at most 0.0063.
Values sent between devices are 32-bit elements; how exact they have to be, the bound alone decides.
No kernel may reach another device: no remote copies, remote signals or barrier semaphores. Data moves between devices by JAX's collectives and lax.ppermute only.
A program may use at most 64 MiB of HBM per device.

v0:
```python
import jax
import jax.numpy as jnp
from jax import lax
from jax.sharding import PartitionSpec as P

BLK = 30


def with_halo(array, sides, width):
    for axis, dim in sides:
        size, length = (lax.axis_size(axis), array.shape[dim])
        up = [(i, (i + 1) % size) for i in range(size)]
        down = [(j, i) for i, j in up]
        last = lax.slice_in_dim(array, length - width, length, axis=dim)
        initial = lax.slice_in_dim(array, 0, width, axis=dim)
        before = lax.ppermute(last, axis, up)
        after = lax.ppermute(initial, axis, down)
        array = jnp.concatenate([before, array, after], axis=dim)
    return array


def assemble_x(copies):
    padded = with_halo(copies, (("gx", 0),), 1)
    return copies + jnp.stack([padded[0], jnp.zeros_like(padded[0]), padded[4]], 0)


def assemble_y(copies):
    padded = with_halo(copies, (("gy", 1),), 1)
    return copies + jnp.stack([padded[:, 0], jnp.zeros_like(padded[:, 0]), padded[:, 4]], 1)


def gather_faces(along_x, along_y):
    return jnp.stack([along_x[0:2], along_x[1:3], along_y[:, 0:2], along_y[:, 1:3]], 2)


def on_device(
    resid_x,
    resid_y,
    face_weights,
    face_counts,
    neumann,
    schur,
    basis,
    coarse_map,
    column_inverse,
    column_basis,
    top_inverse,
):
    high = lax.Precision.HIGHEST
    face_dofs = resid_x.shape[3]
    loads = resid_x.shape[4]
    inner = neumann.shape[3]
    coarse_local = basis.shape[4]
    column_size = column_inverse.shape[3]
    dof_index = jnp.arange(face_dofs, dtype=jnp.int32)
    live = (dof_index[None, None, None, :] < face_counts[:, :, 0, :, None] * BLK).astype(
        jnp.float32
    )
    scale = face_weights[:, :, 0] * live
    assembled_x = assemble_x(resid_x)[:, :, 0]
    assembled_y = assemble_y(resid_y)[:, :, 0]
    faces = gather_faces(assembled_x, assembled_y)
    upart = (faces * scale[..., None]).reshape(4, inner, loads).astype(jnp.bfloat16)
    neumann_flat = neumann.reshape(4, inner, inner)
    basis_flat = basis.reshape(4, inner, coarse_local)
    wpart = jnp.einsum("snk,skr->snr", neumann_flat, upart, preferred_element_type=jnp.float32)
    gpart = jnp.einsum("snc,snr->scr", basis_flat, upart, preferred_element_type=jnp.float32)
    targets = coarse_map.reshape(4 * coarse_local)
    onehot = (targets[:, None] == jnp.arange(column_size, dtype=jnp.int32)[None, :]).astype(
        jnp.float32
    )
    column_part = lax.dot_general(
        onehot, gpart.reshape(4 * coarse_local, loads), (((0,), (0,)), ((), ())), precision=high
    )
    column_res = lax.psum(column_part, "gz")
    inverse_rows = column_inverse[0, 0]
    basis_rows = column_basis[0, 0]
    row_count = inverse_rows.shape[0]
    row_start = lax.axis_index("gz") * row_count
    own_rows = lax.dynamic_slice_in_dim(column_res, row_start, row_count, 0)
    level_two = jnp.dot(inverse_rows, column_res, precision=high)
    top_part = lax.dot_general(basis_rows, own_rows, (((0,), (0,)), ((), ())), precision=high)
    column_top = lax.psum(top_part, "gz")
    top_res = lax.psum(column_top, ("gx", "gy"))
    level_three = jnp.dot(top_inverse, top_res, precision=high)
    value_rows = level_two + jnp.dot(basis_rows, level_three, precision=high)
    column_vals = lax.all_gather(value_rows, "gz", axis=0, tiled=True)
    coarse_vals = (
        jnp.dot(onehot, column_vals, precision=high)
        .reshape(4, coarse_local, loads)
        .astype(jnp.bfloat16)
    )
    ypart = wpart + jnp.einsum(
        "snc,scr->snr", basis_flat, coarse_vals, preferred_element_type=jnp.float32
    )
    contrib = ypart.reshape(2, 2, 4, face_dofs, loads) * scale[..., None]
    send_x = jnp.stack(
        [contrib[0, :, 0], contrib[0, :, 1] + contrib[1, :, 0], contrib[1, :, 1]], 0
    )[:, :, None]
    send_y = jnp.stack(
        [contrib[:, 0, 2], contrib[:, 0, 3] + contrib[:, 1, 2], contrib[:, 1, 3]], 1
    )[:, :, None]
    z_x = assemble_x(send_x)
    z_y = assemble_y(send_y)
    zfaces = gather_faces(z_x[:, :, 0], z_y[:, :, 0])
    zsub = (zfaces * live[..., None]).reshape(4, inner, loads).astype(jnp.bfloat16)
    image = jnp.einsum(
        "snk,skr->snr", schur.reshape(4, inner, inner), zsub, preferred_element_type=jnp.float32
    )
    return (z_x, z_y, image.astype(jnp.bfloat16).reshape(2, 2, 1, inner, loads))


def solution(mesh):
    return jax.shard_map(
        on_device,
        mesh=mesh,
        in_specs=(
            P("gx", "gy", "gz", None, None),
            P("gx", "gy", "gz", None, None),
            P("gx", "gy", "gz", None, None),
            P("gx", "gy", "gz", None),
            P("gx", "gy", "gz", None, None),
            P("gx", "gy", "gz", None, None),
            P("gx", "gy", "gz", None, None),
            P("gx", "gy", "gz", None),
            P("gx", "gy", "gz", None),
            P("gx", "gy", "gz", None),
            P(),
        ),
        out_specs=(
            P("gx", "gy", "gz", None, None),
            P("gx", "gy", "gz", None, None),
            P("gx", "gy", "gz", None, None),
        ),
        check_vma=False,
    )
```

profile of v0, /device:TPU:6, one launch (start us, length us, event | category | flops | bytes accessed | tf_op | source)
XLA Modules:
  0.0 522.4 jit_solution(4546723145671781828)
XLA Ops:
  7.2 2.4 fusion.25
  9.6 2.2 collective-permute-start.2
  11.9 0.8 copy.74
  12.7 0.8 copy.75
  14.6 0.6 reduce.3
  15.8 7.1 %collective-permute-done.2 = f32[2,1,1,120,512]{4,3,1,0,2:T(8,128)} collective-permute-done((f32[2,1,1,120,512]{4,3,1,0,2:T(8,128)}, f32[2,1,1,120,512]{4,3,1,0,2:T(8,128)}, u32[]{:S(2)}, u32[]{:S(2)}) %collective-permute-start.2) | collective-permute-done | bytes 491552 | tf_op jit(solution)/shard_map/ppermute | solution.py:16
  22.9 1.2 collective-permute-done.3
  24.1 1.5 fusion.3
  25.9 1.1 copy-done.6
  27.0 1.5 maximum_add_fusion
  30.2 1.0 copy-done.2
  31.2 1.7 fusion.8
  33.0 153.5 %all-reduce.4.cloned.1.call-done = f32[512,512]{1,0:T(8,128)} async-done(((f32[512,512]{1,0:T(8,128)}), f32[512,512]{1,0:T(8,128)}) %all-reduce.4.cloned.1.call-update) | async-done | bytes 1048592 | tf_op jit(solution)/shard_map/psum | solution.py:75
  186.5 2.8 convolution_bitcast_fusion
  189.4 148.8 %all-reduce.6.cloned.1.call-done = f32[512,512]{0,1:T(8,128)} async-done(((f32[512,512]{0,1:T(8,128)}), f32[512,512]{0,1:T(8,128)}) %all-reduce.6.cloned.1.call-update) | async-done | bytes 1048592 | tf_op jit(solution)/shard_map/psum | solution.py:83
  338.5 0.7 fusion.15
  339.2 64.1 %all-reduce.8.cloned.1.call-done = f32[512,512]{0,1:T(8,128)} async-done(((f32[512,512]{0,1:T(8,128)}), f32[512,512]{0,1:T(8,128)}) %all-reduce.8.cloned.1.call-update) | async-done | bytes 1048592 | tf_op jit(solution)/shard_map/psum | solution.py:84
  403.3 3.4 fusion.26
  406.7 1.6 fusion.5
  408.4 78.2 %all-gather.2.cloned.1.call-done = f32[512,512]{1,0:T(8,128)} async-done(((f32[16,512]{1,0:T(8,128)}), f32[512,512]{1,0:T(8,128)}) %all-gather.2.cloned.1.call-update) | async-done | bytes 1048592 | tf_op jit(solution)/shard_map/all_gather | solution.py:87
  486.6 2.0 convolution_convert_fusion
  488.6 0.7 fusion.27
  489.3 1.4 copy-done.3
  490.7 1.3 convolution_add_fusion
  494.4 1.5 collective-permute-start.7
  496.2 1.3 copy.68
  497.6 9.4 %collective-permute-done.6 = f32[2,1,1,120,512]{4,3,0,2,1:T(8,128)S(1)} collective-permute-done((f32[2,1,1,120,512]{4,3,0,2,1:T(8,128)S(1)}, f32[2,1,1,120,512]{4,3,0,2,1:T(8,128)S(1)}, u32[]{:S(2)}, u32[]{:S(2)}) %collective-permute-start.6) | collective-permute-done | bytes 491552 | tf_op jit(solution)/shard_map/ppermute | solution.py:16
  507.0 1.5 collective-permute-done.7
  510.3 1.0 copy-done.7
  511.3 2.5 fusion.2
  513.8 1.5 fusion.4
  515.3 0.6 copy-done.1
  (72 shorter events, 8.6 us)
Async XLA Ops:
  7.2 482.1 %copy-start = (bf16[2,2,1,480,480]{4,3,2,1,0:T(8,128)(2,1)S(1)}, bf16[2,2,1,480,480]{4,3,2,1,0:T(8,128)(2,1)}, u32[]{:S(2)}) copy-start(bf16[2,2,1,480,480]{4,3,2,1,0:T(8,128)(2,1)} %param.15) | copy-start | bytes 5529604
  7.2 4.6 copy-start.5
  7.2 179.3 %all-reduce.4.cloned.1.call-start = ((), (), s32[]{:S(2)}) async-start(), calls=%async_computation | async-start | bytes 2097152 | tf_op jit(solution)/shard_map/psum | solution.py:75
  9.6 13.3 %collective-permute-start.2 = (f32[2,1,1,120,512]{4,3,1,0,2:T(8,128)}, f32[2,1,1,120,512]{4,3,1,0,2:T(8,128)}, u32[]{:S(2)}, u32[]{:S(2)}) collective-permute-start(f32[2,1,1,120,512]{4,3,1,0,2:T(8,128)} %get-tuple-element.35), channel_id=1, source_target_pairs={{0,32},{32,64},{64,96},{96,0},{1,33},{33,65},{65,97},{97,1},{2,34}... | collective-permute-start | bytes 1474568 | tf_op jit(solution)/shard_map/ppermute | solution.py:16
  11.8 12.3 %collective-permute-start.3 = (f32[2,1,1,120,512]{4,3,1,0,2:T(8,128)}, f32[2,1,1,120,512]{4,3,1,0,2:T(8,128)}, u32[]{:S(2)}, u32[]{:S(2)}) collective-permute-start(f32[2,1,1,120,512]{4,3,1,0,2:T(8,128)} %get-tuple-element.36), channel_id=1, source_target_pairs={{32,0},{64,32},{96,64},{0,96},{33,1},{65,33},{97,65},{1,97},{34,2}... | collective-permute-start | bytes 1474568 | tf_op jit(solution)/shard_map/ppermute | solution.py:17
  11.9 2.2 copy-start.13
  11.9 2.7 copy-start.14
  11.9 3.7 copy-start.12
  11.9 12.2 %copy-start.4 = (f32[2,3,1,120,512]{4,3,2,1,0:T(8,128)S(1)}, f32[2,3,1,120,512]{4,3,2,1,0:T(8,128)}, u32[]{:S(2)}) copy-start(f32[2,3,1,120,512]{4,3,2,1,0:T(8,128)} %param.12) | copy-start | bytes 4423684
  12.7 13.1 %collective-permute-start.1 = (f32[1,2,1,120,512]{4,3,0,1,2:T(8,128)}, f32[1,2,1,120,512]{4,3,0,1,2:T(8,128)}, u32[]{:S(2)}, u32[]{:S(2)}) collective-permute-start(f32[1,2,1,120,512]{4,3,0,1,2:T(8,128)} %copy.74), channel_id=1, source_target_pairs={{128,0},{0,128},{129,1},{1,129},{130,2},{2,130},{131,3},{3,131},{1... | collective-permute-start | bytes 1474568 | tf_op jit(solution)/shard_map/ppermute | solution.py:17
  13.5 12.3 %collective-permute-start = (f32[1,2,1,120,512]{4,3,0,1,2:T(8,128)}, f32[1,2,1,120,512]{4,3,0,1,2:T(8,128)}, u32[]{:S(2)}, u32[]{:S(2)}) collective-permute-start(f32[1,2,1,120,512]{4,3,0,1,2:T(8,128)} %copy.75), channel_id=1, source_target_pairs={{0,128},{128,0},{1,129},{129,1},{2,130},{130,2},{3,131},{131,3},{4... | collective-permute-start | bytes 1474568 | tf_op jit(solution)/shard_map/ppermute | solution.py:16
  25.6 1.4 copy-start.6
  28.7 1.0 copy-start.9
  29.3 1.9 copy-start.2
  31.2 155.3 %copy-start.10 = (f32[1,1,16,512]{3,2,1,0:T(8,128)S(1)}, f32[1,1,16,512]{3,2,1,0:T(8,128)}, u32[]{:S(2)}) copy-start(f32[1,1,16,512]{3,2,1,0:T(8,128)} %param.20) | copy-start | bytes 98308
  32.9 305.4 %all-reduce.6.cloned.1.call-start = ((), (), s32[]{:S(2)}) async-start(), calls=%async_computation.1 | async-start | bytes 2097152 | tf_op jit(solution)/shard_map/psum | solution.py:83
  33.0 305.6 %copy-start.11 = (f32[1,1,16,512]{3,2,1,0:T(8,128)S(1)}, f32[1,1,16,512]{3,2,1,0:T(8,128)}, u32[]{:S(2)}) copy-start(f32[1,1,16,512]{3,2,1,0:T(8,128)} %param.19) | copy-start | bytes 98308
  186.5 152.0 %copy-start.8 = (f32[512,512]{1,0:T(8,128)S(1)}, f32[512,512]{1,0:T(8,128)}, u32[]{:S(2)}) copy-start(f32[512,512]{1,0:T(8,128)} %all-reduce.4.cloned.1.call-done) | copy-start | bytes 3145732
  189.4 213.9 %all-reduce.8.cloned.1.call-start = ((), (), s32[]{:S(2)}) async-start(), calls=%async_computation.2 | async-start | bytes 2097152 | tf_op jit(solution)/shard_map/psum | solution.py:84
  338.3 148.3 %all-gather.2.cloned.1.call-start = ((), (), s32[]{:S(2)}) async-start(), calls=%async_computation.3 | async-start | bytes 1081344 | tf_op jit(solution)/shard_map/all_gather | solution.py:87
  488.5 2.1 copy-start.3
  492.5 3.3 collective-permute-start.5
  492.6 3.2 collective-permute-start.4
  493.7 13.3 %collective-permute-start.6 = (f32[2,1,1,120,512]{4,3,0,2,1:T(8,128)S(1)}, f32[2,1,1,120,512]{4,3,0,2,1:T(8,128)S(1)}, u32[]{:S(2)}, u32[]{:S(2)}) collective-permute-start(f32[2,1,1,120,512]{4,3,0,2,1:T(8,128)S(1)} %get-tuple-element.27), channel_id=1, source_target_pairs={{0,32},{32,64},{64,96},{96,0},{1,33},{33,65},{65,97},{97,1},{2,34}... | collective-permute-start | bytes 1474568 | tf_op jit(solution)/shard_map/ppermute | solution.py:16
  494.4 14.2 %collective-permute-start.7 = (f32[2,1,1,120,512]{4,3,0,2,1:T(8,128)S(1)}, f32[2,1,1,120,512]{4,3,0,2,1:T(8,128)S(1)}, u32[]{:S(2)}, u32[]{:S(2)}) collective-permute-start(f32[2,1,1,120,512]{4,3,0,2,1:T(8,128)S(1)} %get-tuple-element.28), channel_id=1, source_target_pairs={{32,0},{64,32},{96,64},{0,96},{33,1},{65,33},{97,65},{1,97},{34,2}... | collective-permute-start | bytes 1474568 | tf_op jit(solution)/shard_map/ppermute | solution.py:17
  509.7 1.5 copy-start.7
  513.8 2.1 copy-start.1
Sparse Core Ops, SparseCore 0:
  33.0 153.4 all-reduce.3
  190.5 147.6 all-reduce.5
  340.6 62.6 all-reduce.7
  408.4 78.0 all-gather.1
where the time goes:
time: 523 us; the launch traced here: 522 us
  waiting for transfers between devices  464 us (89%)
  matrix products  17.2 us (3%)
  between operations  14.1 us (3%)
  local copies, waits for them, and re-layouts  13.3 us (3%)
  other arithmetic  8.02 us (2%)
  starting transfers between devices  5.73 us (1%)
    psum x1, waiting for transfers between devices, on_device(): column_res = lax.psum(column_part, 'gz')  154 us
    psum x1, waiting for transfers between devices, on_device(): column_top = lax.psum(top_part, 'gz')  149 us
    all_gather x1, waiting for transfers between devices, on_device(): column_vals = lax.all_gather(value_rows, 'gz', axis=0, tiled=True)  78.2 us
    psum x1, waiting for transfers between devices, on_device(): top_res = lax.psum(column_top, ('gx', 'gy'))  64.1 us
    ppermute x4, waiting for transfers between devices, with_halo(): before = lax.ppermute(last, axis, up)  16.6 us
  transfers between devices with their start and end apart: 12, of which 8 were waited for; matrix products, arithmetic and copies ran while one was open for 2% of the time, Pallas kernels for 0%

commit v1 on v0

--- a/solution.py
+++ b/solution.py
@@ -84,7 +84,9 @@
     top_res = lax.psum(column_top, ("gx", "gy"))
     level_three = jnp.dot(top_inverse, top_res, precision=high)
     value_rows = level_two + jnp.dot(basis_rows, level_three, precision=high)
-    column_vals = lax.all_gather(value_rows, "gz", axis=0, tiled=True)
+    column_vals = jnp.concatenate(
+        lax.all_to_all(jnp.stack([value_rows] * lax.axis_size("gz")), "gz", 0, 0), axis=0
+    )
     coarse_vals = (
         jnp.dot(onehot, column_vals, precision=high)
         .reshape(4, coarse_local, loads)

time: 523 us -> 483 us (0.924)
  waiting for transfers between devices: 464 us -> 415 us
  starting transfers between devices: 5.73 us -> 15.5 us
    all_gather x1 -> x0, waiting for transfers between devices: 78.2 us -> none  [on_device(): column_vals = lax.all_gather(value_rows, 'gz', axis=0, tiled=True)]
    all_to_all x0 -> x1, waiting for transfers between devices: none -> 28.8 us  [on_device(): lax.all_to_all(jnp.stack([value_rows] * lax.axis_size('gz')), 'gz', 0, 0)]
    all_to_all x0 -> x1, starting transfers between devices: none -> 10 us  [on_device(): lax.all_to_all(jnp.stack([value_rows] * lax.axis_size('gz')), 'gz', 0, 0)]
where the time goes in v1:
time: 483 us; the launch traced here: 482 us
  waiting for transfers between devices  415 us (86%)
  starting transfers between devices  15.5 us (3%)
  matrix products  15.4 us (3%)
  local copies, waits for them, and re-layouts  14.4 us (3%)
  between operations  14.1 us (3%)
  other arithmetic  8.02 us (2%)
    psum x1, waiting for transfers between devices, on_device(): column_res = lax.psum(column_part, 'gz')  153 us
    psum x1, waiting for transfers between devices, on_device(): column_top = lax.psum(top_part, 'gz')  149 us
    psum x1, waiting for transfers between devices, on_device(): top_res = lax.psum(column_top, ('gx', 'gy'))  64.3 us
    all_to_all x1, waiting for transfers between devices, on_device(): lax.all_to_all(jnp.stack([value_rows] * lax.axis_size('gz')), 'gz', 0, 0)  28.8 us
    ppermute x4, waiting for transfers between devices, with_halo(): before = lax.ppermute(last, axis, up)  16.6 us
    all_to_all x1, starting transfers between devices, on_device(): lax.all_to_all(jnp.stack([value_rows] * lax.axis_size('gz')), 'gz', 0, 0)  10 us
  transfers between devices with their start and end apart: 12, of which 8 were waited for; matrix products, arithmetic and copies ran while one was open for 2% of the time, Pallas kernels for 0%

profile of v1, /device:TPU:6, one launch (start us, length us, event | category | flops | bytes accessed | tf_op | source)
XLA Modules:
  0.0 482.1 jit_solution(9640983474781880057)
XLA Ops:
  7.2 2.4 fusion.27
  9.6 2.2 collective-permute-start.2
  11.9 0.8 copy.54
  12.7 0.8 copy.55
  15.7 7.2 %collective-permute-done.2 = f32[2,1,1,120,512]{4,3,1,0,2:T(8,128)} collective-permute-done((f32[2,1,1,120,512]{4,3,1,0,2:T(8,128)}, f32[2,1,1,120,512]{4,3,1,0,2:T(8,128)}, u32[]{:S(2)}, u32[]{:S(2)}) %collective-permute-start.2) | collective-permute-done | bytes 491552 | tf_op jit(solution)/shard_map/ppermute | solution.py:16
  22.9 1.2 collective-permute-done.3
  24.1 1.5 fusion.3
  25.9 1.1 copy-done.6
  27.0 1.5 maximum_add_fusion
  30.2 1.0 copy-done.2
  31.2 1.7 fusion.10
  33.0 153.5 %all-reduce.4.cloned.1.call-done = f32[512,512]{1,0:T(8,128)} async-done(((f32[512,512]{1,0:T(8,128)}), f32[512,512]{1,0:T(8,128)}) %all-reduce.4.cloned.1.call-update) | async-done | bytes 1048592 | tf_op jit(solution)/shard_map/psum | solution.py:75
  186.5 2.8 convolution_bitcast_fusion
  189.4 148.8 %all-reduce.6.cloned.1.call-done = f32[512,512]{0,1:T(8,128)} async-done(((f32[512,512]{0,1:T(8,128)}), f32[512,512]{0,1:T(8,128)}) %all-reduce.6.cloned.1.call-update) | async-done | bytes 1048592 | tf_op jit(solution)/shard_map/psum | solution.py:83
  338.3 0.7 fusion.17
  338.9 64.3 %all-reduce.8.cloned.1.call-done = f32[512,512]{0,1:T(8,128)} async-done(((f32[512,512]{0,1:T(8,128)}), f32[512,512]{0,1:T(8,128)}) %all-reduce.8.cloned.1.call-update) | async-done | bytes 1048592 | tf_op jit(solution)/shard_map/psum | solution.py:84
  403.2 3.4 fusion.28
  406.6 1.0 fusion.5
  407.6 1.1 stack.46
  408.7 10.0 %all-to-all-start = ((f32[32,16,512]{2,1,0:T(8,128)}), f32[32,16,512]{2,1,0:T(8,128)S(1)}, u32[]{:S(2)}, u32[]{:S(2)}) async-start(f32[32,16,512]{2,1,0:T(8,128)} %stack.46), calls=%async_computation | async-start | bytes 2097152 | tf_op jit(solution)/shard_map/all_to_all | solution.py:88
  418.9 28.8 %all-to-all-done = f32[32,16,512]{2,1,0:T(8,128)S(1)} async-done(((f32[32,16,512]{2,1,0:T(8,128)}), f32[32,16,512]{2,1,0:T(8,128)S(1)}, u32[]{:S(2)}, u32[]{:S(2)}) %all-to-all-start) | async-done | bytes 1048608 | tf_op jit(solution)/shard_map/all_to_all | solution.py:88
  447.7 0.7 convolution_convert_fusion
  448.4 0.7 fusion.29
  449.2 1.4 copy-done.3
  450.5 1.3 convolution_add_fusion
  453.7 2.0 collective-permute-start.7
  456.0 1.3 copy.48
  457.5 9.4 %collective-permute-done.6 = f32[2,1,1,120,512]{4,3,0,2,1:T(8,128)S(1)} collective-permute-done((f32[2,1,1,120,512]{4,3,0,2,1:T(8,128)S(1)}, f32[2,1,1,120,512]{4,3,0,2,1:T(8,128)S(1)}, u32[]{:S(2)}, u32[]{:S(2)}) %collective-permute-start.6) | collective-permute-done | bytes 491552 | tf_op jit(solution)/shard_map/ppermute | solution.py:16
  466.9 1.3 collective-permute-done.7
  470.0 1.0 copy-done.7
  470.9 2.5 fusion.2
  473.5 1.5 fusion.4
  (72 shorter events, 9.0 us)
Async XLA Ops:
  7.2 442.0 %copy-start = (bf16[2,2,1,480,480]{4,3,2,1,0:T(8,128)(2,1)S(1)}, bf16[2,2,1,480,480]{4,3,2,1,0:T(8,128)(2,1)}, u32[]{:S(2)}) copy-start(bf16[2,2,1,480,480]{4,3,2,1,0:T(8,128)(2,1)} %param.15) | copy-start | bytes 5529604
  7.2 4.6 copy-start.5
  7.2 179.3 %all-reduce.4.cloned.1.call-start = ((), (), s32[]{:S(2)}) async-start(), calls=%async_computation.1 | async-start | bytes 2097152 | tf_op jit(solution)/shard_map/psum | solution.py:75
  9.6 13.3 %collective-permute-start.2 = (f32[2,1,1,120,512]{4,3,1,0,2:T(8,128)}, f32[2,1,1,120,512]{4,3,1,0,2:T(8,128)}, u32[]{:S(2)}, u32[]{:S(2)}) collective-permute-start(f32[2,1,1,120,512]{4,3,1,0,2:T(8,128)} %get-tuple-element.32), channel_id=1, source_target_pairs={{0,32},{32,64},{64,96},{96,0},{1,33},{33,65},{65,97},{97,1},{2,34}... | collective-permute-start | bytes 1474568 | tf_op jit(solution)/shard_map/ppermute | solution.py:16
  11.8 12.3 %collective-permute-start.3 = (f32[2,1,1,120,512]{4,3,1,0,2:T(8,128)}, f32[2,1,1,120,512]{4,3,1,0,2:T(8,128)}, u32[]{:S(2)}, u32[]{:S(2)}) collective-permute-start(f32[2,1,1,120,512]{4,3,1,0,2:T(8,128)} %get-tuple-element.33), channel_id=1, source_target_pairs={{32,0},{64,32},{96,64},{0,96},{33,1},{65,33},{97,65},{1,97},{34,2}... | collective-permute-start | bytes 1474568 | tf_op jit(solution)/shard_map/ppermute | solution.py:17
  11.9 2.2 copy-start.14
  11.9 2.7 copy-start.13
  11.9 3.7 copy-start.12
  11.9 12.2 %copy-start.4 = (f32[2,3,1,120,512]{4,3,2,1,0:T(8,128)S(1)}, f32[2,3,1,120,512]{4,3,2,1,0:T(8,128)}, u32[]{:S(2)}) copy-start(f32[2,3,1,120,512]{4,3,2,1,0:T(8,128)} %param.12) | copy-start | bytes 4423684
  12.7 13.1 %collective-permute-start.1 = (f32[1,2,1,120,512]{4,3,0,1,2:T(8,128)}, f32[1,2,1,120,512]{4,3,0,1,2:T(8,128)}, u32[]{:S(2)}, u32[]{:S(2)}) collective-permute-start(f32[1,2,1,120,512]{4,3,0,1,2:T(8,128)} %copy.54), channel_id=1, source_target_pairs={{128,0},{0,128},{129,1},{1,129},{130,2},{2,130},{131,3},{3,131},{1... | collective-permute-start | bytes 1474568 | tf_op jit(solution)/shard_map/ppermute | solution.py:17
  13.5 12.3 %collective-permute-start = (f32[1,2,1,120,512]{4,3,0,1,2:T(8,128)}, f32[1,2,1,120,512]{4,3,0,1,2:T(8,128)}, u32[]{:S(2)}, u32[]{:S(2)}) collective-permute-start(f32[1,2,1,120,512]{4,3,0,1,2:T(8,128)} %copy.55), channel_id=1, source_target_pairs={{0,128},{128,0},{1,129},{129,1},{2,130},{130,2},{3,131},{131,3},{4... | collective-permute-start | bytes 1474568 | tf_op jit(solution)/shard_map/ppermute | solution.py:16
  25.6 1.4 copy-start.6
  28.7 1.0 copy-start.9
  29.3 1.9 copy-start.2
  31.2 155.3 %copy-start.10 = (f32[1,1,16,512]{3,2,1,0:T(8,128)S(1)}, f32[1,1,16,512]{3,2,1,0:T(8,128)}, u32[]{:S(2)}) copy-start(f32[1,1,16,512]{3,2,1,0:T(8,128)} %param.20) | copy-start | bytes 98308
  32.9 305.3 %all-reduce.6.cloned.1.call-start = ((), (), s32[]{:S(2)}) async-start(), calls=%async_computation.2 | async-start | bytes 2097152 | tf_op jit(solution)/shard_map/psum | solution.py:83
  33.0 305.3 %copy-start.11 = (f32[1,1,16,512]{3,2,1,0:T(8,128)S(1)}, f32[1,1,16,512]{3,2,1,0:T(8,128)}, u32[]{:S(2)}) copy-start(f32[1,1,16,512]{3,2,1,0:T(8,128)} %param.19) | copy-start | bytes 98308
  186.5 151.8 %copy-start.8 = (f32[512,512]{1,0:T(8,128)S(1)}, f32[512,512]{1,0:T(8,128)}, u32[]{:S(2)}) copy-start(f32[512,512]{1,0:T(8,128)} %all-reduce.4.cloned.1.call-done) | copy-start | bytes 3145732
  189.3 213.9 %all-reduce.8.cloned.1.call-start = ((), (), s32[]{:S(2)}) async-start(), calls=%async_computation.3 | async-start | bytes 2097152 | tf_op jit(solution)/shard_map/psum | solution.py:84
  408.7 38.9 %all-to-all-start = ((f32[32,16,512]{2,1,0:T(8,128)}), f32[32,16,512]{2,1,0:T(8,128)S(1)}, u32[]{:S(2)}, u32[]{:S(2)}) async-start(f32[32,16,512]{2,1,0:T(8,128)} %stack.46), calls=%async_computation | async-start | bytes 2097152 | tf_op jit(solution)/shard_map/all_to_all | solution.py:88
  448.4 2.1 copy-start.3
  452.4 3.3 collective-permute-start.5
  452.5 3.2 collective-permute-start.4
  453.6 13.3 %collective-permute-start.6 = (f32[2,1,1,120,512]{4,3,0,2,1:T(8,128)S(1)}, f32[2,1,1,120,512]{4,3,0,2,1:T(8,128)S(1)}, u32[]{:S(2)}, u32[]{:S(2)}) collective-permute-start(f32[2,1,1,120,512]{4,3,0,2,1:T(8,128)S(1)} %get-tuple-element.24), channel_id=1, source_target_pairs={{0,32},{32,64},{64,96},{96,0},{1,33},{33,65},{65,97},{97,1},{2,34}... | collective-permute-start | bytes 1474568 | tf_op jit(solution)/shard_map/ppermute | solution.py:16
  453.7 14.5 %collective-permute-start.7 = (f32[2,1,1,120,512]{4,3,0,2,1:T(8,128)S(1)}, f32[2,1,1,120,512]{4,3,0,2,1:T(8,128)S(1)}, u32[]{:S(2)}, u32[]{:S(2)}) collective-permute-start(f32[2,1,1,120,512]{4,3,0,2,1:T(8,128)S(1)} %get-tuple-element.25), channel_id=1, source_target_pairs={{32,0},{64,32},{96,64},{0,96},{33,1},{65,33},{97,65},{1,97},{34,2}... | collective-permute-start | bytes 1474568 | tf_op jit(solution)/shard_map/ppermute | solution.py:17
  469.4 1.5 copy-start.7
  473.5 2.1 copy-start.1
Sparse Core Ops, SparseCore 0:
  33.0 153.3 all-reduce.3
  190.5 147.6 all-reduce.5
  340.6 62.6 all-reduce.7
